TPU v7x, 32 devices: a whole 2x2x4 slice. The times are simulated.
32 devices in a mesh: gx: 8 (over z, core), gy: 4 (over y, x).
Axes of the slice: x: 2, y: 2, z: 4, core: 2. Of those that a mesh axis runs over, the one named last changes fastest.
Arguments:
- density: float32 [128, 192, 128], P('gx', 'gy'), may hold values from -6 to 6
- momenta: float32 [3, 128, 192, 128], P(None, 'gx', 'gy'), may hold values from -6 to 6
- smooth_taps: float32 [33], replicated, may hold values from -1 to 1
- deriv_taps: float32 [33], replicated, may hold values from -1 to 1
- kick_step: float32 [], replicated, may hold values from 0.5 to 1.5
Outputs:
- kicked: float32 [3, 128, 192, 128], P(None, 'gx', 'gy')
All inputs are finite; a program needn't handle non-finite values.
Results may differ from a plain program's by a relative error of at most 0.00007.
Values sent between devices are 32-bit elements; how exact they have to be, the bound alone decides.
No kernel may reach another device: no remote copies, remote signals or barrier semaphores. Data moves between devices by JAX's collectives and lax.ppermute only.
A program may use at most 64 MiB of HBM per device.

v0:
```python
import math
import jax
import jax.numpy as jnp
from jax import lax
from jax.sharding import PartitionSpec as P

FACTOR = 4
LONG_COUPLING = 16.0
HIGHEST = lax.Precision.HIGHEST


def extended(cells, sides, width):
    for axis, dim in sides:
        count = lax.axis_size(axis)
        head = lax.slice_in_dim(cells, 0, width, axis=dim)
        tail = lax.slice_in_dim(cells, cells.shape[dim] - width, cells.shape[dim], axis=dim)
        cells = jnp.concatenate(
            [
                lax.ppermute(tail, axis, [(i, (i + 1) % count) for i in range(count)]),
                cells,
                lax.ppermute(head, axis, [((i + 1) % count, i) for i in range(count)]),
            ],
            axis=dim,
        )
    return cells


def band_matrix(weights, sources, targets, shift, period):
    source_idx = lax.broadcasted_iota(jnp.int32, (sources, targets), 0)
    target_idx = lax.broadcasted_iota(jnp.int32, (sources, targets), 1)
    offset = source_idx - target_idx + shift
    if period > 0:
        offset = offset % period
    tap_index = jnp.arange(weights.shape[0], dtype=jnp.int32)
    one_hot = (offset[:, :, None] == tap_index[None, None, :]).astype(jnp.float32)
    return jnp.einsum("abt,t->ab", one_hot, weights, precision=HIGHEST)


def contract(values, along, matrix):
    result = jnp.tensordot(values, matrix, axes=((along,), (0,)), precision=HIGHEST)
    return jnp.moveaxis(result, -1, along)


def dft_table(period, sources, targets):
    product = sources[:, None] * targets[None, :] % period
    phases = 2.0 * math.pi / period * product.astype(jnp.float32)
    return (jnp.cos(phases), jnp.sin(phases))


def transform(spectrum, along, table, orient):
    cosine, sine_part = table
    real_part = contract(spectrum[0], along, cosine) - orient * contract(
        spectrum[1], along, sine_part
    )
    imag_part = contract(spectrum[1], along, cosine) + orient * contract(
        spectrum[0], along, sine_part
    )
    return jnp.stack([real_part, imag_part])


def spectral(spectrum, wave_x, wave_y, wave_z, count_x, count_y, count_z):
    phase_x = 2.0 * math.pi / count_x * wave_x.astype(jnp.float32)
    phase_y = 2.0 * math.pi / count_y * wave_y.astype(jnp.float32)
    phase_z = 2.0 * math.pi / count_z * wave_z.astype(jnp.float32)
    laplace = (
        (2.0 - 2.0 * jnp.cos(phase_x))[:, None, None]
        + (2.0 - 2.0 * jnp.cos(phase_y))[None, :, None]
        + (2.0 - 2.0 * jnp.cos(phase_z))[None, None, :]
    )
    anchor = (
        (wave_x[:, None, None] == 0) & (wave_y[None, :, None] == 0) & (wave_z[None, None, :] == 0)
    )
    weight_k = jnp.where(anchor, 0.0, 1.0 / jnp.where(anchor, 1.0, laplace)) / float(
        count_x * count_y * count_z
    )
    sine_list = [
        jnp.sin(phase_x)[:, None, None],
        jnp.sin(phase_y)[None, :, None],
        jnp.sin(phase_z)[None, None, :],
    ]
    real_part = jnp.stack([-sine_part * spectrum[1] * weight_k for sine_part in sine_list])
    imag_part = jnp.stack([sine_part * spectrum[0] * weight_k for sine_part in sine_list])
    return jnp.stack([real_part, imag_part])


def short_forces(density, smooth_taps, deriv_taps):
    radius = (smooth_taps.shape[0] - 1) // 2
    padded = extended(density, (("gx", 0), ("gy", 1)), radius)
    rows_in = padded.shape[0]
    smooth_rows = band_matrix(smooth_taps, rows_in, rows_in - 2 * radius, 0, 0)
    deriv_rows = band_matrix(deriv_taps, rows_in, rows_in - 2 * radius, 0, 0)
    smooth_x = jnp.einsum("jyz,ji->iyz", padded, smooth_rows, precision=HIGHEST)
    deriv_x = jnp.einsum("jyz,ji->iyz", padded, deriv_rows, precision=HIGHEST)
    cols_in = smooth_x.shape[1]
    smooth_cols = band_matrix(smooth_taps, cols_in, cols_in - 2 * radius, 0, 0)
    deriv_cols = band_matrix(deriv_taps, cols_in, cols_in - 2 * radius, 0, 0)
    depth = density.shape[2]
    smooth_depth = band_matrix(smooth_taps, depth, depth, radius, depth)
    deriv_depth = band_matrix(deriv_taps, depth, depth, radius, depth)
    first = jnp.einsum("xjz,ji->xiz", deriv_x, smooth_cols, precision=HIGHEST)
    second = jnp.einsum("xjz,ji->xiz", smooth_x, deriv_cols, precision=HIGHEST)
    third = jnp.einsum("xjz,ji->xiz", smooth_x, smooth_cols, precision=HIGHEST)
    return jnp.stack(
        [
            jnp.einsum("xyj,ji->xyi", first, smooth_depth, precision=HIGHEST),
            jnp.einsum("xyj,ji->xyi", second, smooth_depth, precision=HIGHEST),
            jnp.einsum("xyj,ji->xyi", third, deriv_depth, precision=HIGHEST),
        ]
    )


def long_forces(density):
    tile_x = density.shape[0] // FACTOR
    tile_y = density.shape[1] // FACTOR
    tile_z = density.shape[2] // FACTOR
    coarse = density.reshape(tile_x, FACTOR, tile_y, FACTOR, tile_z, FACTOR).mean(axis=(1, 3, 5))
    count_x = tile_x * lax.axis_size("gx")
    count_y = tile_y * lax.axis_size("gy")
    depth_all = jnp.arange(tile_z, dtype=jnp.int32)
    depth_table = dft_table(tile_z, depth_all, depth_all)
    spectrum = jnp.stack(
        [contract(coarse, 2, depth_table[0]), -contract(coarse, 2, depth_table[1])]
    )
    cols_all = jnp.arange(count_y, dtype=jnp.int32)
    cols_table = dft_table(count_y, cols_all, cols_all)
    spectrum = lax.all_gather(spectrum, "gy", axis=2, tiled=True)
    spectrum = transform(spectrum, 1, cols_table, -1.0)
    spectrum = lax.all_to_all(spectrum, "gx", split_axis=2, concat_axis=1, tiled=True)
    rows_all = jnp.arange(count_x, dtype=jnp.int32)
    rows_table = dft_table(count_x, rows_all, rows_all)
    spectrum = transform(spectrum, 0, rows_table, -1.0)
    wave_y = lax.axis_index("gx") * spectrum.shape[2] + jnp.arange(
        spectrum.shape[2], dtype=jnp.int32
    )
    wave_z = jnp.arange(spectrum.shape[3], dtype=jnp.int32)
    fields = spectral(spectrum, rows_all, wave_y, wave_z, count_x, count_y, tile_z)
    fields = transform(fields, 1, rows_table, 1.0)
    fields = lax.all_to_all(fields, "gx", split_axis=2, concat_axis=3, tiled=True)
    mine = lax.axis_index("gy") * tile_y + jnp.arange(tile_y, dtype=jnp.int32)
    fields = transform(fields, 2, dft_table(count_y, cols_all, mine), 1.0)
    return contract(fields[0], 3, depth_table[0]) - contract(fields[1], 3, depth_table[1])


def per_device(density, momenta, smooth_taps, deriv_taps, kick_step):
    long_range = long_forces(density)
    short_range = short_forces(density, smooth_taps, deriv_taps)
    fine_long = jnp.repeat(jnp.repeat(jnp.repeat(long_range, FACTOR, 1), FACTOR, 2), FACTOR, 3)
    forces = short_range + LONG_COUPLING * fine_long
    return momenta + kick_step * forces


def solution(mesh):
    in_specs = (P("gx", "gy", None), P(None, "gx", "gy", None), P(), P(), P())
    out_specs = P(None, "gx", "gy", None)
    return jax.shard_map(
        per_device, mesh=mesh, in_specs=in_specs, out_specs=out_specs, check_vma=False
    )
```

profile of v0, /device:TPU:0, one launch (start us, length us, event | category | flops | bytes accessed | tf_op | source)
XLA Modules:
  0.0 103.8 jit_solution(2877908469738453902)
XLA Ops:
  0.0 1.1 %copy.173 = f32[16,48,128]{2,0,1:T(8,128)S(1)} copy(f32[16,48,128]{2,1,0:T(8,128)} %param.5) | data formatting | bytes 786432 | tf_op args[0]
  1.1 0.5 collective-permute-start
  1.7 4.1 %collective-permute-start.1 = (f32[16,48,128]{2,0,1:T(8,128)S(1)}, f32[16,48,128]{2,0,1:T(8,128)S(1)}, u32[]{:S(2)}, u32[]{:S(2)}) collective-permute-start(f32[16,48,128]{2,0,1:T(8,128)S(1)} %copy.173), channel_id=1, source_target_pairs={{4,0},{8,4},{12,8},{16,12},{20,16},{24,20},{28,24},{0,28},{5,1},{9... | collective-permute-start | bytes 1179656 | tf_op jit(solution)/shard_map/ppermute | solution.py:21
  5.8 15.2 %reshape.181 = f32[4,4,12,4,32,4]{5,4,3,2,1,0:T(8,128)} reshape(f32[16,48,128]{2,1,0:T(8,128)} %param.5) | data formatting | bytes 786432 | tf_op jit(solution)/shard_map/reshape | solution.py:116
  20.9 5.6 %reduce_sum.9 = f32[4,12,32]{2,1,0:T(8,128)S(1)} reduce(f32[4,4,12,4,32,4]{5,4,3,2,1,0:T(8,128)} %reshape.181, f32[]{:T(128)} %constant.82.clone.1), dimensions={1,3,5}, to_apply=%region_0.0 | reduce | flops 96768 | bytes 399364 | tf_op jit(solution)/shard_map/reduce_sum | solution.py:116
  27.0 9.3 %all_gather.3 = f32[2,4,48,32]{3,1,0,2:T(4,128)S(1)} all-gather(f32[2,4,12,32]{3,1,0,2:T(4,128)S(1)} %copy.179), channel_id=1, replica_groups=mesh['gx'=8,'gy'=4] {'gy'}, dimensions={2}, use_global_device_ids=true | all-gather | bytes 61440 | tf_op jit(solution)/shard_map/all_gather | solution.py:126
  38.0 0.8 reshape.212
  38.8 3.5 %all-to-all-start = ((f32[8,1,1536]{2,1,0:T(1,128)}), f32[8,1,1536]{2,1,0:T(1,128)S(1)}, u32[]{:S(2)}, u32[]{:S(2)}) async-start(f32[8,1,1536]{2,1,0:T(1,128)} %reshape.212), calls=%async_computation | async-start | bytes 98304 | tf_op jit(solution)/shard_map/all_to_all | solution.py:128
  42.7 0.9 fusion.24
  43.7 0.9 fusion.23
  44.6 1.0 select_reduce_fusion.1
  45.9 1.9 %fusion = f32[1,128,128]{2,0,1:T(1,128)} fusion(pred[128,128,33]{1,0,2:T(32,128)(4,1)S(1)} %iota_compare_fusion, f32[33]{0:T(128)S(1)} %copy-done.10), kind=kOutput, calls=%fused_computation | convolution fusion | flops 6488064 | bytes 606340 | tf_op jit(solution)/shard_map/abt,t->ab/dot_general | solution.py:36
  48.1 0.5 broadcast.337
  48.6 0.7 reduce.4
  49.9 0.4 fusion.72
  50.3 0.4 fusion.13
  50.6 0.4 multiply_bitcast_fusion.5
  51.0 0.6 fusion.27
  51.7 0.6 fusion.26
  52.3 0.6 fusion.9
  53.0 0.6 fusion.8
  54.1 1.3 %reshape.214 = f32[8,1,4608]{2,1,0:T(1,128)} reshape(f32[32,3,6,2,32]{4,3,2,1,0:T(2,128)S(1)} %bitcast.198) | data formatting | bytes 294912
  55.3 4.8 %all-to-all-start.1 = ((f32[8,1,4608]{2,1,0:T(1,128)}), f32[8,1,4608]{2,1,0:T(1,128)S(1)}, u32[]{:S(2)}, u32[]{:S(2)}) async-start(f32[8,1,4608]{2,1,0:T(1,128)} %reshape.214), calls=%async_computation.1 | async-start | bytes 294912 | tf_op jit(solution)/shard_map/all_to_all | solution.py:138
  60.8 1.9 %fusion.2 = f32[1,128,128]{2,0,1:T(1,128)} fusion(pred[128,128,33]{1,0,2:T(32,128)(4,1)S(1)} %iota_compare_fusion, f32[33]{0:T(128)S(1)} %copy-done.11), kind=kOutput, calls=%fused_computation.2 | convolution fusion | flops 6488064 | bytes 606340 | tf_op jit(solution)/shard_map/abt,t->ab/dot_general | solution.py:36
  62.8 4.4 %all-to-all-done.1 = f32[8,1,4608]{2,1,0:T(1,128)S(1)} async-done(((f32[8,1,4608]{2,1,0:T(1,128)}), f32[8,1,4608]{2,1,0:T(1,128)S(1)}, u32[]{:S(2)}, u32[]{:S(2)}) %all-to-all-start.1) | async-done | bytes 147488 | tf_op jit(solution)/shard_map/all_to_all | solution.py:138
  67.1 0.9 reduce.5
  68.0 0.5 reshape.215
  69.1 0.9 fusion.95
  70.0 1.0 fusion.11
  71.0 1.0 fusion.97
  71.9 1.0 fusion.12
  73.1 1.0 fusion.227
  74.1 1.4 %collective-permute-start.2 = (f32[48,16,128]{2,0,1:T(8,128)}, f32[48,16,128]{2,0,1:T(8,128)S(1)}, u32[]{:S(2)}, u32[]{:S(2)}) collective-permute-start(f32[48,16,128]{2,0,1:T(8,128)} %get-tuple-element.7), channel_id=1, source_target_pairs={{0,1},{1,2},{2,3},{3,0},{4,5},{5,6},{6,7},{7,4},{8,9},{9,10},{10,1... | collective-permute-start | bytes 1179656 | tf_op jit(solution)/shard_map/ppermute | solution.py:19
  75.5 1.6 %collective-permute-start.3 = (f32[48,16,128]{2,0,1:T(8,128)}, f32[48,16,128]{2,0,1:T(8,128)}, u32[]{:S(2)}, u32[]{:S(2)}) collective-permute-start(f32[48,16,128]{2,0,1:T(8,128)} %get-tuple-element.8), channel_id=1, source_target_pairs={{1,0},{2,1},{3,2},{0,3},{5,4},{6,5},{7,6},{4,7},{9,8},{10,9},{11,1... | collective-permute-start | bytes 1179656 | tf_op jit(solution)/shard_map/ppermute | solution.py:21
  77.9 1.5 %copy.203 = f32[3,16,48,32]{2,1,3,0:T(8,128)} copy(f32[3,16,48,32]{3,1,2,0:T(8,128)S(1)} %bitcast.196) | data formatting | bytes 589824 | tf_op jit(solution)/shard_map/mul | solution.py:148
  79.4 1.4 %broadcast_in_dim.14 = f32[3,16,48,32,4]{2,1,4,3,0:T(8,128)S(1)} broadcast(f32[3,16,48,32]{2,1,3,0:T(8,128)} %copy.203), dimensions={0,1,2,3} | broadcast | bytes 1474560 | tf_op jit(solution)/shard_map/broadcast_in_dim | solution.py:147
  80.8 1.9 %copy.204 = f32[3,16,48,128]{3,2,1,0:T(8,128)} copy(f32[3,16,48,128]{2,1,3,0:T(8,128)S(1)} %bitcast.195) | data formatting | bytes 2359296 | tf_op jit(solution)/shard_map/mul | solution.py:148
  82.7 4.5 %collective-permute-done.2 = f32[48,16,128]{2,0,1:T(8,128)S(1)} collective-permute-done((f32[48,16,128]{2,0,1:T(8,128)}, f32[48,16,128]{2,0,1:T(8,128)S(1)}, u32[]{:S(2)}, u32[]{:S(2)}) %collective-permute-start.2) | collective-permute-done | bytes 393248 | tf_op jit(solution)/shard_map/ppermute | solution.py:19
  87.2 7.0 %collective-permute-done.3 = f32[48,16,128]{2,0,1:T(8,128)} collective-permute-done((f32[48,16,128]{2,0,1:T(8,128)}, f32[48,16,128]{2,0,1:T(8,128)}, u32[]{:S(2)}, u32[]{:S(2)}) %collective-permute-start.3) | collective-permute-done | bytes 393248 | tf_op jit(solution)/shard_map/ppermute | solution.py:21
  94.2 2.5 %fusion.4 = f32[16,80,128]{2,0,1:T(8,128)S(1)} fusion(f32[48,16,128]{2,0,1:T(8,128)} %collective-permute-done.3, f32[48,48,128]{2,0,1:T(8,128)} %copy-done, f32[48,16,128]{2,0,1:T(8,128)S(1)} %collective-permute-done.2, f32[48,16]{1,0:T(8,128)} %get-tuple-element.6), kind=kOutput, calls=%fused_computation.6 | convolution fusion | flops 95354880 | bytes 2624512 | tf_op jit(solution)/shard_map/jyz,ji->iyz/dot_general | solution.py:92
  96.7 0.7 convolution_bitcast_fusion.1
  97.4 0.7 convolution_bitcast_fusion.3
  98.1 2.1 %fusion.5 = f32[16,80,128]{2,0,1:T(8,128)S(1)} fusion(f32[48,16,128]{2,0,1:T(8,128)} %collective-permute-done.3, f32[48,48,128]{2,0,1:T(8,128)S(1)} %copy-done.1, f32[48,16,128]{2,0,1:T(8,128)S(1)} %collective-permute-done.2, f32[48,16]{1,0:T(8,128)S(1)} %copy-done.6), kind=kOutput, calls=%fused_computation.7 | convolution fusion | flops 95354880 | bytes 2624512 | tf_op jit(solution)/shard_map/jyz,ji->iyz/dot_general | solution.py:93
  100.2 0.7 convolution_bitcast_fusion.5
  101.0 0.5 convolution_bitcast_fusion.2
  101.4 0.5 convolution_bitcast_fusion.4
  101.9 0.5 convolution_bitcast_fusion
  102.6 1.2 %fusion.7 = f32[3,16,48,128]{3,2,1,0:T(8,128)} fusion(f32[3,16,48,128]{3,2,1,0:T(8,128)S(1)} %copy-done.4, f32[3,16,48,128]{3,2,1,0:T(8,128)S(1)} %copy-done.2, f32[1,16,48,128]{3,2,1,0:T(8,128)S(1)} %convolution_bitcast_fusion, f32[1,16,48,128]{3,2,1,0:T(8,128)S(1)} %convolution_bitcast_fusion.2, f32[1,16,48,128]{3,2,1,0:T(8,128)S(1)} %convolution_bitcast_fusion.4, ...), kind=kLoop, calls=%fused_computation.16 | loop fusion | flops 1474560 | bytes 4718596 | tf_op jit(solution)/shard_map/add | solution.py:149
  (76 shorter events, 5.6 us)
Async XLA Ops:
  1.1 71.8 %collective-permute-start = (f32[16,48,128]{2,0,1:T(8,128)S(1)}, f32[16,48,128]{2,0,1:T(8,128)S(1)}, u32[]{:S(2)}, u32[]{:S(2)}) collective-permute-start(f32[16,48,128]{2,0,1:T(8,128)S(1)} %copy.173), channel_id=1, source_target_pairs={{0,4},{4,8},{8,12},{12,16},{16,20},{20,24},{24,28},{28,0},{1,5},{5... | collective-permute-start | bytes 1179656 | tf_op jit(solution)/shard_map/ppermute | solution.py:19
  1.7 71.4 %collective-permute-start.1 = (f32[16,48,128]{2,0,1:T(8,128)S(1)}, f32[16,48,128]{2,0,1:T(8,128)S(1)}, u32[]{:S(2)}, u32[]{:S(2)}) collective-permute-start(f32[16,48,128]{2,0,1:T(8,128)S(1)} %copy.173), channel_id=1, source_target_pairs={{4,0},{8,4},{12,8},{16,12},{20,16},{24,20},{28,24},{0,28},{5,1},{9... | collective-permute-start | bytes 1179656 | tf_op jit(solution)/shard_map/ppermute | solution.py:21
  36.4 6.3 %copy-start.11 = (f32[33]{0:T(128)S(1)}, f32[33]{0:T(128)}, u32[]{:S(2)}) copy-start(f32[33]{0:T(128)} %param.7) | copy-start | bytes 400
  37.2 6.5 %copy-start.10 = (f32[33]{0:T(128)S(1)}, f32[33]{0:T(128)}, u32[]{:S(2)}) copy-start(f32[33]{0:T(128)} %param.8) | copy-start | bytes 400
  38.8 9.2 %all-to-all-start = ((f32[8,1,1536]{2,1,0:T(1,128)}), f32[8,1,1536]{2,1,0:T(1,128)S(1)}, u32[]{:S(2)}, u32[]{:S(2)}) async-start(f32[8,1,1536]{2,1,0:T(1,128)} %reshape.212), calls=%async_computation | async-start | bytes 98304 | tf_op jit(solution)/shard_map/all_to_all | solution.py:128
  55.3 11.8 %all-to-all-start.1 = ((f32[8,1,4608]{2,1,0:T(1,128)}), f32[8,1,4608]{2,1,0:T(1,128)S(1)}, u32[]{:S(2)}, u32[]{:S(2)}) async-start(f32[8,1,4608]{2,1,0:T(1,128)} %reshape.214), calls=%async_computation.1 | async-start | bytes 294912 | tf_op jit(solution)/shard_map/all_to_all | solution.py:138
  69.1 3.9 %copy-start.3 = (f32[16,48,128]{2,1,0:T(8,128)S(1)}, f32[16,48,128]{2,1,0:T(8,128)}, u32[]{:S(2)}) copy-start(f32[16,48,128]{2,1,0:T(8,128)} %param.5) | copy-start | bytes 1179652
  73.1 4.7 %copy-start = (f32[48,48,128]{2,0,1:T(8,128)}, f32[48,48,128]{2,0,1:T(8,128)S(1)}, u32[]{:S(2)}) copy-start(f32[48,48,128]{2,0,1:T(8,128)S(1)} %constant_dynamic-update-slice_fusion) | copy-start | bytes 3538948
  74.1 13.1 %collective-permute-start.2 = (f32[48,16,128]{2,0,1:T(8,128)}, f32[48,16,128]{2,0,1:T(8,128)S(1)}, u32[]{:S(2)}, u32[]{:S(2)}) collective-permute-start(f32[48,16,128]{2,0,1:T(8,128)} %get-tuple-element.7), channel_id=1, source_target_pairs={{0,1},{1,2},{2,3},{3,0},{4,5},{5,6},{6,7},{7,4},{8,9},{9,10},{10,1... | collective-permute-start | bytes 1179656 | tf_op jit(solution)/shard_map/ppermute | solution.py:19
  75.5 18.7 %collective-permute-start.3 = (f32[48,16,128]{2,0,1:T(8,128)}, f32[48,16,128]{2,0,1:T(8,128)}, u32[]{:S(2)}, u32[]{:S(2)}) collective-permute-start(f32[48,16,128]{2,0,1:T(8,128)} %get-tuple-element.8), channel_id=1, source_target_pairs={{1,0},{2,1},{3,2},{0,3},{5,4},{6,5},{7,6},{4,7},{9,8},{10,9},{11,1... | collective-permute-start | bytes 1179656 | tf_op jit(solution)/shard_map/ppermute | solution.py:21
  94.2 2.5 %copy-start.7 = (f32[1,80,48]{1,0,2:T(1,128)S(1)}, f32[1,80,48]{1,0,2:T(1,128)}, u32[]{:S(2)}) copy-start(f32[1,80,48]{1,0,2:T(1,128)} %fusion.24) | copy-start | bytes 46084
  94.2 3.2 %copy-start.9 = (f32[1,80,48]{1,0,2:T(1,128)S(1)}, f32[1,80,48]{1,0,2:T(1,128)}, u32[]{:S(2)}) copy-start(f32[1,80,48]{1,0,2:T(1,128)} %fusion.23) | copy-start | bytes 46084
  96.7 1.4 %copy-start.1 = (f32[48,48,128]{2,0,1:T(8,128)S(1)}, f32[48,48,128]{2,0,1:T(8,128)}, u32[]{:S(2)}) copy-start(f32[48,48,128]{2,0,1:T(8,128)} %copy-done) | copy-start | bytes 3538948
  96.7 1.4 %copy-start.6 = (f32[48,16]{1,0:T(8,128)S(1)}, f32[48,16]{1,0:T(8,128)}, u32[]{:S(2)}) copy-start(f32[48,16]{1,0:T(8,128)} %get-tuple-element.5) | copy-start | bytes 9220
  98.1 2.8 %copy-start.5 = (f32[1,128,128]{2,0,1:T(1,128)S(1)}, f32[1,128,128]{2,0,1:T(1,128)}, u32[]{:S(2)}) copy-start(f32[1,128,128]{2,0,1:T(1,128)} %fusion.2) | copy-start | bytes 196612
  100.2 1.7 %copy-start.8 = (f32[1,128,128]{2,0,1:T(1,128)S(1)}, f32[1,128,128]{2,0,1:T(1,128)}, u32[]{:S(2)}) copy-start(f32[1,128,128]{2,0,1:T(1,128)} %fusion) | copy-start | bytes 196612
  100.9 1.4 %copy-start.2 = (f32[3,16,48,128]{3,2,1,0:T(8,128)S(1)}, f32[3,16,48,128]{3,2,1,0:T(8,128)}, u32[]{:S(2)}) copy-start(f32[3,16,48,128]{3,2,1,0:T(8,128)} %copy.204) | copy-start | bytes 3538948
  100.9 1.6 %copy-start.4 = (f32[3,16,48,128]{3,2,1,0:T(8,128)S(1)}, f32[3,16,48,128]{3,2,1,0:T(8,128)}, u32[]{:S(2)}) copy-start(f32[3,16,48,128]{3,2,1,0:T(8,128)} %param.6) | copy-start | bytes 3538948
where the time goes:
time: 104 us
  local copies, waits for them, and re-layouts  27.2 us (26%)
  matrix products  24 us (23%)
  starting transfers between devices  15.9 us (15%)
  waiting for transfers between devices  15.8 us (15%)
  other arithmetic  10.2 us (10%)
  blocking collectives  9.29 us (9%)
  between operations  1.3 us (1%)
    reshape x1, local copies, waits for them, and re-layouts, long_forces(): density.reshape(tile_x, FACTOR, tile_y, FACTOR, tile_z, FACTOR)  15.2 us
    dot_general x20, matrix products, contract(): jnp.tensordot(values, matrix, axes=((along,), (0,)), precision=HIGHEST)  10.2 us
    all_gather x1, blocking collectives, long_forces(): spectrum = lax.all_gather(spectrum, 'gy', axis=2, tiled=True)  9.29 us
    ppermute x2, waiting for transfers between devices, extended(): lax.ppermute(head, axis, [((i + 1) % count, i) for i in range(count)])  6.97 us
    dot_general x4, matrix products, band_matrix(): return jnp.einsum('abt,t->ab', one_hot, weights, precision=HIGHEST)  5.77 us
    ppermute x2, starting transfers between devices, extended(): lax.ppermute(head, axis, [((i + 1) % count, i) for i in range(count)])  5.65 us
    reduce_sum x1, other arithmetic, long_forces(): density.reshape(tile_x, FACTOR, tile_y, FACTOR, tile_z, FACTOR)  5.57 us
    all_to_all x1, starting transfers between devices, long_forces(): lax.all_to_all(fields, 'gx', split_axis=2, concat_axis=3, tiled=True)  4.85 us
  transfers between devices with their start and end apart: 6, of which 3 were waited for; matrix products, arithmetic and copies ran while one was open for 48% of the time, Pallas kernels for 0%

commit v1 on v0

--- a/solution.py
+++ b/solution.py
@@ -7,6 +7,12 @@
 FACTOR = 4
 LONG_COUPLING = 16.0
 HIGHEST = lax.Precision.HIGHEST
+
+
+def all_parts(x, name, along):
+    parts = lax.all_gather(x, name, axis=0, tiled=False)
+    result = jnp.concatenate(parts, axis=along)
+    return result
 
 
 def extended(cells, sides, width):
@@ -123,7 +129,7 @@
     )
     cols_all = jnp.arange(count_y, dtype=jnp.int32)
     cols_table = dft_table(count_y, cols_all, cols_all)
-    spectrum = lax.all_gather(spectrum, "gy", axis=2, tiled=True)
+    spectrum = all_parts(spectrum, "gy", 2)
     spectrum = transform(spectrum, 1, cols_table, -1.0)
     spectrum = lax.all_to_all(spectrum, "gx", split_axis=2, concat_axis=1, tiled=True)
     rows_all = jnp.arange(count_x, dtype=jnp.int32)

time: 104 us -> 104 us (level)
    unnamed x33 -> x31, local copies, waits for them, and re-layouts: 4.37 us -> 4.21 us
where the time goes in v1:
time: 104 us
  local copies, waits for them, and re-layouts  27.2 us (26%)
  matrix products  24 us (23%)
  starting transfers between devices  15.9 us (15%)
  waiting for transfers between devices  15.8 us (15%)
  other arithmetic  10.2 us (10%)
  blocking collectives  9.29 us (9%)
  between operations  1.31 us (1%)
    reshape x1, local copies, waits for them, and re-layouts, long_forces(): density.reshape(tile_x, FACTOR, tile_y, FACTOR, tile_z, FACTOR)  15.2 us
    dot_general x20, matrix products, contract(): jnp.tensordot(values, matrix, axes=((along,), (0,)), precision=HIGHEST)  10.2 us
    all_gather x1, blocking collectives, all_parts(): parts = lax.all_gather(x, name, axis=0, tiled=False)  9.29 us
    ppermute x2, waiting for transfers between devices, extended(): lax.ppermute(head, axis, [((i + 1) % count, i) for i in range(count)])  6.97 us
    dot_general x4, matrix products, band_matrix(): return jnp.einsum('abt,t->ab', one_hot, weights, precision=HIGHEST)  5.77 us
    ppermute x2, starting transfers between devices, extended(): lax.ppermute(head, axis, [((i + 1) % count, i) for i in range(count)])  5.65 us
    reduce_sum x1, other arithmetic, long_forces(): density.reshape(tile_x, FACTOR, tile_y, FACTOR, tile_z, FACTOR)  5.57 us
    all_to_all x1, starting transfers between devices, long_forces(): lax.all_to_all(fields, 'gx', split_axis=2, concat_axis=3, tiled=True)  4.84 us
  transfers between devices with their start and end apart: 6, of which 3 were waited for; matrix products, arithmetic and copies ran while one was open for 48% of the time, Pallas kernels for 0%

profile of v1, /device:TPU:0, one launch (start us, length us, event | category | flops | bytes accessed | tf_op | source)
XLA Modules:
  0.0 103.8 jit_solution(3766774510523758043)
XLA Ops:
  0.0 1.1 %copy.182 = f32[16,48,128]{2,0,1:T(8,128)S(1)} copy(f32[16,48,128]{2,1,0:T(8,128)} %param.5) | data formatting | bytes 786432 | tf_op args[0]
  1.1 0.5 collective-permute-start
  1.7 4.1 %collective-permute-start.1 = (f32[16,48,128]{2,0,1:T(8,128)S(1)}, f32[16,48,128]{2,0,1:T(8,128)S(1)}, u32[]{:S(2)}, u32[]{:S(2)}) collective-permute-start(f32[16,48,128]{2,0,1:T(8,128)S(1)} %copy.182), channel_id=1, source_target_pairs={{4,0},{8,4},{12,8},{16,12},{20,16},{24,20},{28,24},{0,28},{5,1},{9... | collective-permute-start | bytes 1179656 | tf_op jit(solution)/shard_map/ppermute | solution.py:27
  5.8 15.2 %reshape.189 = f32[4,4,12,4,32,4]{5,4,3,2,1,0:T(8,128)} reshape(f32[16,48,128]{2,1,0:T(8,128)} %param.5) | data formatting | bytes 786432 | tf_op jit(solution)/shard_map/reshape | solution.py:122
  20.9 5.6 %reduce_sum.9 = f32[4,12,32]{2,1,0:T(8,128)S(1)} reduce(f32[4,4,12,4,32,4]{5,4,3,2,1,0:T(8,128)} %reshape.189, f32[]{:T(128)} %constant.82.clone.1), dimensions={1,3,5}, to_apply=%region_0.0 | reduce | flops 96768 | bytes 399364 | tf_op jit(solution)/shard_map/reduce_sum | solution.py:122
  27.0 9.3 %all-gather = f32[8,4,12,32]{3,1,2,0:T(4,128)S(1)} all-gather(f32[2,4,12,32]{3,1,2,0:T(4,128)S(1)} %copy.188), channel_id=2, replica_groups=mesh['gx'=8,'gy'=4] {'gy'}, dimensions={0}, use_global_device_ids=true | all-gather | bytes 61440 | tf_op jit(solution)/shard_map/all_gather | solution.py:13
  38.0 0.8 reshape.222
  38.8 3.5 %all-to-all-start = ((f32[8,1,1536]{2,1,0:T(1,128)}), f32[8,1,1536]{2,1,0:T(1,128)S(1)}, u32[]{:S(2)}, u32[]{:S(2)}) async-start(f32[8,1,1536]{2,1,0:T(1,128)} %reshape.222), calls=%async_computation | async-start | bytes 98304 | tf_op jit(solution)/shard_map/all_to_all | solution.py:134
  42.7 0.9 fusion.24
  43.7 0.9 fusion.23
  44.6 1.0 select_reduce_fusion.1
  45.9 1.9 %fusion = f32[1,128,128]{2,0,1:T(1,128)} fusion(pred[128,128,33]{1,0,2:T(32,128)(4,1)S(1)} %iota_compare_fusion, f32[33]{0:T(128)S(1)} %copy-done.10), kind=kOutput, calls=%fused_computation | convolution fusion | flops 6488064 | bytes 606340 | tf_op jit(solution)/shard_map/abt,t->ab/dot_general | solution.py:42
  48.1 0.5 broadcast.337
  48.6 0.7 reduce.4
  49.5 0.4 fusion.65
  50.3 0.4 fusion.13
  50.7 0.4 multiply_bitcast_fusion.5
  51.1 0.6 fusion.27
  51.7 0.6 fusion.26
  52.4 0.6 fusion.9
  53.0 0.6 fusion.8
  54.1 1.3 %reshape.224 = f32[8,1,4608]{2,1,0:T(1,128)} reshape(f32[32,3,6,2,32]{4,3,2,1,0:T(2,128)S(1)} %bitcast.198) | data formatting | bytes 294912
  55.3 4.8 %all-to-all-start.1 = ((f32[8,1,4608]{2,1,0:T(1,128)}), f32[8,1,4608]{2,1,0:T(1,128)S(1)}, u32[]{:S(2)}, u32[]{:S(2)}) async-start(f32[8,1,4608]{2,1,0:T(1,128)} %reshape.224), calls=%async_computation.1 | async-start | bytes 294912 | tf_op jit(solution)/shard_map/all_to_all | solution.py:144
  60.8 1.9 %fusion.2 = f32[1,128,128]{2,0,1:T(1,128)} fusion(pred[128,128,33]{1,0,2:T(32,128)(4,1)S(1)} %iota_compare_fusion, f32[33]{0:T(128)S(1)} %copy-done.11), kind=kOutput, calls=%fused_computation.2 | convolution fusion | flops 6488064 | bytes 606340 | tf_op jit(solution)/shard_map/abt,t->ab/dot_general | solution.py:42
  62.8 4.4 %all-to-all-done.1 = f32[8,1,4608]{2,1,0:T(1,128)S(1)} async-done(((f32[8,1,4608]{2,1,0:T(1,128)}), f32[8,1,4608]{2,1,0:T(1,128)S(1)}, u32[]{:S(2)}, u32[]{:S(2)}) %all-to-all-start.1) | async-done | bytes 147488 | tf_op jit(solution)/shard_map/all_to_all | solution.py:144
  67.1 0.9 reduce.5
  68.0 0.5 reshape.225
  69.1 0.9 fusion.91
  70.0 1.0 fusion.11
  71.0 1.0 fusion.93
  71.9 1.0 fusion.12
  73.2 1.0 fusion.223
  74.1 1.4 %collective-permute-start.2 = (f32[48,16,128]{2,0,1:T(8,128)}, f32[48,16,128]{2,0,1:T(8,128)S(1)}, u32[]{:S(2)}, u32[]{:S(2)}) collective-permute-start(f32[48,16,128]{2,0,1:T(8,128)} %get-tuple-element.7), channel_id=1, source_target_pairs={{0,1},{1,2},{2,3},{3,0},{4,5},{5,6},{6,7},{7,4},{8,9},{9,10},{10,1... | collective-permute-start | bytes 1179656 | tf_op jit(solution)/shard_map/ppermute | solution.py:25
  75.5 1.6 %collective-permute-start.3 = (f32[48,16,128]{2,0,1:T(8,128)}, f32[48,16,128]{2,0,1:T(8,128)}, u32[]{:S(2)}, u32[]{:S(2)}) collective-permute-start(f32[48,16,128]{2,0,1:T(8,128)} %get-tuple-element.8), channel_id=1, source_target_pairs={{1,0},{2,1},{3,2},{0,3},{5,4},{6,5},{7,6},{4,7},{9,8},{10,9},{11,1... | collective-permute-start | bytes 1179656 | tf_op jit(solution)/shard_map/ppermute | solution.py:27
  77.9 1.5 %copy.215 = f32[3,16,48,32]{2,1,3,0:T(8,128)} copy(f32[3,16,48,32]{3,1,2,0:T(8,128)S(1)} %bitcast.196) | data formatting | bytes 589824 | tf_op jit(solution)/shard_map/mul | solution.py:154
  79.4 1.4 %broadcast_in_dim.14 = f32[3,16,48,32,4]{2,1,4,3,0:T(8,128)S(1)} broadcast(f32[3,16,48,32]{2,1,3,0:T(8,128)} %copy.215), dimensions={0,1,2,3} | broadcast | bytes 1474560 | tf_op jit(solution)/shard_map/broadcast_in_dim | solution.py:153
  80.8 1.9 %copy.216 = f32[3,16,48,128]{3,2,1,0:T(8,128)} copy(f32[3,16,48,128]{2,1,3,0:T(8,128)S(1)} %bitcast.195) | data formatting | bytes 2359296 | tf_op jit(solution)/shard_map/mul | solution.py:154
  82.7 4.5 %collective-permute-done.2 = f32[48,16,128]{2,0,1:T(8,128)S(1)} collective-permute-done((f32[48,16,128]{2,0,1:T(8,128)}, f32[48,16,128]{2,0,1:T(8,128)S(1)}, u32[]{:S(2)}, u32[]{:S(2)}) %collective-permute-start.2) | collective-permute-done | bytes 393248 | tf_op jit(solution)/shard_map/ppermute | solution.py:25
  87.2 7.0 %collective-permute-done.3 = f32[48,16,128]{2,0,1:T(8,128)} collective-permute-done((f32[48,16,128]{2,0,1:T(8,128)}, f32[48,16,128]{2,0,1:T(8,128)}, u32[]{:S(2)}, u32[]{:S(2)}) %collective-permute-start.3) | collective-permute-done | bytes 393248 | tf_op jit(solution)/shard_map/ppermute | solution.py:27
  94.2 2.5 %fusion.4 = f32[16,80,128]{2,0,1:T(8,128)S(1)} fusion(f32[48,16,128]{2,0,1:T(8,128)} %collective-permute-done.3, f32[48,48,128]{2,0,1:T(8,128)} %copy-done, f32[48,16,128]{2,0,1:T(8,128)S(1)} %collective-permute-done.2, f32[48,16]{1,0:T(8,128)} %get-tuple-element.6), kind=kOutput, calls=%fused_computation.6 | convolution fusion | flops 95354880 | bytes 2624512 | tf_op jit(solution)/shard_map/jyz,ji->iyz/dot_general | solution.py:98
  96.7 0.7 convolution_bitcast_fusion.1
  97.4 0.7 convolution_bitcast_fusion.3
  98.1 2.1 %fusion.5 = f32[16,80,128]{2,0,1:T(8,128)S(1)} fusion(f32[48,16,128]{2,0,1:T(8,128)} %collective-permute-done.3, f32[48,48,128]{2,0,1:T(8,128)S(1)} %copy-done.1, f32[48,16,128]{2,0,1:T(8,128)S(1)} %collective-permute-done.2, f32[48,16]{1,0:T(8,128)S(1)} %copy-done.6), kind=kOutput, calls=%fused_computation.7 | convolution fusion | flops 95354880 | bytes 2624512 | tf_op jit(solution)/shard_map/jyz,ji->iyz/dot_general | solution.py:99
  100.2 0.7 convolution_bitcast_fusion.5
  101.0 0.5 convolution_bitcast_fusion.2
  101.4 0.5 convolution_bitcast_fusion.4
  101.9 0.5 convolution_bitcast_fusion
  102.6 1.2 %fusion.7 = f32[3,16,48,128]{3,2,1,0:T(8,128)} fusion(f32[3,16,48,128]{3,2,1,0:T(8,128)S(1)} %copy-done.4, f32[3,16,48,128]{3,2,1,0:T(8,128)S(1)} %copy-done.2, f32[1,16,48,128]{3,2,1,0:T(8,128)S(1)} %convolution_bitcast_fusion, f32[1,16,48,128]{3,2,1,0:T(8,128)S(1)} %convolution_bitcast_fusion.2, f32[1,16,48,128]{3,2,1,0:T(8,128)S(1)} %convolution_bitcast_fusion.4, ...), kind=kLoop, calls=%fused_computation.16 | loop fusion | flops 1474560 | bytes 4718596 | tf_op jit(solution)/shard_map/add | solution.py:155
  (77 shorter events, 5.6 us)
Async XLA Ops:
  1.1 71.8 %collective-permute-start = (f32[16,48,128]{2,0,1:T(8,128)S(1)}, f32[16,48,128]{2,0,1:T(8,128)S(1)}, u32[]{:S(2)}, u32[]{:S(2)}) collective-permute-start(f32[16,48,128]{2,0,1:T(8,128)S(1)} %copy.182), channel_id=1, source_target_pairs={{0,4},{4,8},{8,12},{12,16},{16,20},{20,24},{24,28},{28,0},{1,5},{5... | collective-permute-start | bytes 1179656 | tf_op jit(solution)/shard_map/ppermute | solution.py:25
  1.7 71.4 %collective-permute-start.1 = (f32[16,48,128]{2,0,1:T(8,128)S(1)}, f32[16,48,128]{2,0,1:T(8,128)S(1)}, u32[]{:S(2)}, u32[]{:S(2)}) collective-permute-start(f32[16,48,128]{2,0,1:T(8,128)S(1)} %copy.182), channel_id=1, source_target_pairs={{4,0},{8,4},{12,8},{16,12},{20,16},{24,20},{28,24},{0,28},{5,1},{9... | collective-permute-start | bytes 1179656 | tf_op jit(solution)/shard_map/ppermute | solution.py:27
  36.4 6.3 %copy-start.11 = (f32[33]{0:T(128)S(1)}, f32[33]{0:T(128)}, u32[]{:S(2)}) copy-start(f32[33]{0:T(128)} %param.7) | copy-start | bytes 400
  37.2 6.5 %copy-start.10 = (f32[33]{0:T(128)S(1)}, f32[33]{0:T(128)}, u32[]{:S(2)}) copy-start(f32[33]{0:T(128)} %param.8) | copy-start | bytes 400
  38.8 9.2 %all-to-all-start = ((f32[8,1,1536]{2,1,0:T(1,128)}), f32[8,1,1536]{2,1,0:T(1,128)S(1)}, u32[]{:S(2)}, u32[]{:S(2)}) async-start(f32[8,1,1536]{2,1,0:T(1,128)} %reshape.222), calls=%async_computation | async-start | bytes 98304 | tf_op jit(solution)/shard_map/all_to_all | solution.py:134
  55.3 11.8 %all-to-all-start.1 = ((f32[8,1,4608]{2,1,0:T(1,128)}), f32[8,1,4608]{2,1,0:T(1,128)S(1)}, u32[]{:S(2)}, u32[]{:S(2)}) async-start(f32[8,1,4608]{2,1,0:T(1,128)} %reshape.224), calls=%async_computation.1 | async-start | bytes 294912 | tf_op jit(solution)/shard_map/all_to_all | solution.py:144
  69.1 3.9 %copy-start.3 = (f32[16,48,128]{2,1,0:T(8,128)S(1)}, f32[16,48,128]{2,1,0:T(8,128)}, u32[]{:S(2)}) copy-start(f32[16,48,128]{2,1,0:T(8,128)} %param.5) | copy-start | bytes 1179652
  73.1 4.7 %copy-start = (f32[48,48,128]{2,0,1:T(8,128)}, f32[48,48,128]{2,0,1:T(8,128)S(1)}, u32[]{:S(2)}) copy-start(f32[48,48,128]{2,0,1:T(8,128)S(1)} %constant_dynamic-update-slice_fusion) | copy-start | bytes 3538948
  74.1 13.1 %collective-permute-start.2 = (f32[48,16,128]{2,0,1:T(8,128)}, f32[48,16,128]{2,0,1:T(8,128)S(1)}, u32[]{:S(2)}, u32[]{:S(2)}) collective-permute-start(f32[48,16,128]{2,0,1:T(8,128)} %get-tuple-element.7), channel_id=1, source_target_pairs={{0,1},{1,2},{2,3},{3,0},{4,5},{5,6},{6,7},{7,4},{8,9},{9,10},{10,1... | collective-permute-start | bytes 1179656 | tf_op jit(solution)/shard_map/ppermute | solution.py:25
  75.5 18.7 %collective-permute-start.3 = (f32[48,16,128]{2,0,1:T(8,128)}, f32[48,16,128]{2,0,1:T(8,128)}, u32[]{:S(2)}, u32[]{:S(2)}) collective-permute-start(f32[48,16,128]{2,0,1:T(8,128)} %get-tuple-element.8), channel_id=1, source_target_pairs={{1,0},{2,1},{3,2},{0,3},{5,4},{6,5},{7,6},{4,7},{9,8},{10,9},{11,1... | collective-permute-start | bytes 1179656 | tf_op jit(solution)/shard_map/ppermute | solution.py:27
  94.2 2.5 %copy-start.7 = (f32[1,80,48]{1,0,2:T(1,128)S(1)}, f32[1,80,48]{1,0,2:T(1,128)}, u32[]{:S(2)}) copy-start(f32[1,80,48]{1,0,2:T(1,128)} %fusion.24) | copy-start | bytes 46084
  94.2 3.2 %copy-start.9 = (f32[1,80,48]{1,0,2:T(1,128)S(1)}, f32[1,80,48]{1,0,2:T(1,128)}, u32[]{:S(2)}) copy-start(f32[1,80,48]{1,0,2:T(1,128)} %fusion.23) | copy-start | bytes 46084
  96.7 1.4 %copy-start.1 = (f32[48,48,128]{2,0,1:T(8,128)S(1)}, f32[48,48,128]{2,0,1:T(8,128)}, u32[]{:S(2)}) copy-start(f32[48,48,128]{2,0,1:T(8,128)} %copy-done) | copy-start | bytes 3538948
  96.7 1.4 %copy-start.6 = (f32[48,16]{1,0:T(8,128)S(1)}, f32[48,16]{1,0:T(8,128)}, u32[]{:S(2)}) copy-start(f32[48,16]{1,0:T(8,128)} %get-tuple-element.5) | copy-start | bytes 9220
  98.1 2.8 %copy-start.5 = (f32[1,128,128]{2,0,1:T(1,128)S(1)}, f32[1,128,128]{2,0,1:T(1,128)}, u32[]{:S(2)}) copy-start(f32[1,128,128]{2,0,1:T(1,128)} %fusion.2) | copy-start | bytes 196612
  100.2 1.7 %copy-start.8 = (f32[1,128,128]{2,0,1:T(1,128)S(1)}, f32[1,128,128]{2,0,1:T(1,128)}, u32[]{:S(2)}) copy-start(f32[1,128,128]{2,0,1:T(1,128)} %fusion) | copy-start | bytes 196612
  100.9 1.4 %copy-start.2 = (f32[3,16,48,128]{3,2,1,0:T(8,128)S(1)}, f32[3,16,48,128]{3,2,1,0:T(8,128)}, u32[]{:S(2)}) copy-start(f32[3,16,48,128]{3,2,1,0:T(8,128)} %copy.216) | copy-start | bytes 3538948
  100.9 1.6 %copy-start.4 = (f32[3,16,48,128]{3,2,1,0:T(8,128)S(1)}, f32[3,16,48,128]{3,2,1,0:T(8,128)}, u32[]{:S(2)}) copy-start(f32[3,16,48,128]{3,2,1,0:T(8,128)} %param.6) | copy-start | bytes 3538948
